TPU v7x, 512 devices: a whole 4x8x8 slice. The times are simulated.
512 devices in a mesh: seq: 64 (over y, x, core), head: 8 (over z).
Axes of the slice: x: 4, y: 8, z: 8, core: 2. Of those that a mesh axis runs over, the one named last changes fastest.
Arguments:
- queries: bfloat16 [32768, 4096], P(('seq', 'head')), may hold values from -5 to 5
- new_keys: bfloat16 [32768, 1024], P(('seq', 'head')), may hold values from -12 to 12
- new_values: bfloat16 [32768, 1024], P(('seq', 'head')), may hold values from -6 to 6
- cache_keys: bfloat16 [131072, 1024], P('seq', 'head'), may hold values from -12 to 12
- cache_values: bfloat16 [131072, 1024], P('seq', 'head'), may hold values from -6 to 6
- tile_lists: int32 [256, 8, 12], P('seq', 'head'), may hold values from 0 to 1023, as said below
Outputs:
- attended: bfloat16 [32768, 4096], P(('seq', 'head'))
Inputs may be any that keep to these rules, and one draw needn't show every extreme that they name: `tile_lists`: for one key head, the 12 tiles of one block's list are distinct; the lists of the 4 blocks of one index of seq together name exactly 24 distinct tiles, at most 2 of them of one index of seq (tiles k * 16 to k * 16 + 15), and some index has exactly 2.
All inputs are finite; a program needn't handle non-finite values.
Results may differ from a plain program's by a relative error of at most 0.003.
Values may be sent and summed in bfloat16 or wider, within the bound.
A program may use at most 64 MiB of HBM per device.

v0:
```python
import math
import jax
import jax.numpy as jnp
from jax import lax
from jax.sharding import PartitionSpec as P

HQ = 32
KV = 8
HD = 128
QB = 128
TILE = 128
SEL = 12
NEG_FILL = -1e30


def passed_along(block, axis, distance):
    devices = range(lax.axis_size(axis))
    route = [(i - distance, i) for i in devices if i - distance in devices]
    return lax.ppermute(block, axis, route)


def pair_ranks(owners, tiles):
    pair_count = owners.shape[-1]
    earlier = jnp.arange(pair_count)[:, None] > jnp.arange(pair_count)[None, :]
    same_tile = tiles[..., :, None] == tiles[..., None, :]
    first_seen = jnp.logical_not(jnp.any(same_tile & earlier, axis=-1))
    same_owner = owners[..., :, None] == owners[..., None, :]
    smaller = tiles[..., None, :] < tiles[..., :, None]
    counted = same_owner & smaller & first_seen[..., None, :]
    return (jnp.sum(counted.astype(jnp.int32), axis=-1), first_seen)


def on_device(queries, new_keys, new_values, cache_keys, cache_values, tile_lists):
    q_rows, k_rows, v_rows = (
        lax.all_to_all(queries, "head", split_axis=1, concat_axis=0, tiled=True),
        lax.all_to_all(new_keys, "head", split_axis=1, concat_axis=0, tiled=True),
        lax.all_to_all(new_values, "head", split_axis=1, concat_axis=0, tiled=True),
    )
    rows_here = q_rows.shape[0]
    kv_here = k_rows.shape[1] // HD
    group_size = HQ // KV
    blocks_here = rows_here // QB
    tiles_here = cache_keys.shape[0] // TILE
    shards = lax.axis_size("seq")
    shard_index = lax.axis_index("seq")
    pair_total = blocks_here * SEL
    pool_size = max(SEL, pair_total // 2)
    capacity = max(2, (4 * pool_size + 3 * shards - 1) // (3 * shards))
    scale_factor = 1.0 / math.sqrt(HD)
    prior_keys, prior_values = passed_along(
        (k_rows[rows_here - QB :], v_rows[rows_here - QB :]), "seq", 1
    )
    pair_tiles = jnp.transpose(tile_lists, (1, 0, 2)).reshape(kv_here, pair_total)
    owners = pair_tiles // tiles_here
    pair_rank, first_seen = pair_ranks(owners, pair_tiles)
    every_list = lax.all_gather(tile_lists, "seq", axis=0, tiled=True)
    every_pair = jnp.transpose(
        every_list.reshape(shards, blocks_here, kv_here, SEL), (0, 2, 1, 3)
    ).reshape(shards, kv_here, pair_total)
    every_owner = every_pair // tiles_here
    every_rank, every_first = pair_ranks(every_owner, every_pair)
    own_hit = ((every_owner == shard_index) & every_first)[..., None]
    rank_hit = every_rank[..., None] == jnp.arange(capacity)
    marked = jnp.where(own_hit & rank_hit, (every_pair % tiles_here)[..., None] + 1, 0)
    asked_ids = jnp.sum(marked, axis=2) - 1
    head_pick = jnp.arange(kv_here)[None, :, None]
    filled = (asked_ids >= 0)[..., None, None]
    safe_ids = jnp.maximum(asked_ids, 0)
    key_tiles = jnp.transpose(cache_keys.reshape(tiles_here, TILE, kv_here, HD), (2, 0, 1, 3))
    value_tiles = jnp.transpose(cache_values.reshape(tiles_here, TILE, kv_here, HD), (2, 0, 1, 3))
    send_keys = jnp.where(filled, key_tiles[head_pick, safe_ids], jnp.zeros((), jnp.bfloat16))
    send_values = jnp.where(filled, value_tiles[head_pick, safe_ids], jnp.zeros((), jnp.bfloat16))
    causal = jnp.arange(QB)[:, None] >= jnp.arange(QB)[None, :]
    head_rows = jnp.arange(kv_here)[:, None]

    def local_part(block_index, source, prior_rows):
        current = lax.dynamic_slice_in_dim(source, block_index * QB, QB, 0)
        before_rows = lax.dynamic_slice_in_dim(source, jnp.maximum(block_index - 1, 0) * QB, QB, 0)
        previous = jnp.where(block_index == 0, prior_rows, before_rows)
        joined = jnp.concatenate([previous, current], axis=0).reshape(2 * QB, kv_here, HD)
        return jnp.transpose(joined, (1, 0, 2))

    def remote_part(block_index, received):
        block_owners = lax.dynamic_slice_in_dim(owners, block_index * SEL, SEL, 1)
        block_ranks = lax.dynamic_slice_in_dim(pair_rank, block_index * SEL, SEL, 1)
        return received[block_owners, head_rows, block_ranks].reshape(kv_here, SEL * TILE, HD)

    def block_weights(block_index, got_keys):
        query_block = lax.dynamic_slice_in_dim(q_rows, block_index * QB, QB, 0).reshape(
            QB, kv_here, group_size, HD
        )
        all_keys = jnp.concatenate(
            [remote_part(block_index, got_keys), local_part(block_index, k_rows, prior_keys)],
            axis=1,
        )
        scores = (
            jnp.einsum("qhgd,hkd->hgqk", query_block, all_keys, preferred_element_type=jnp.float32)
            * scale_factor
        )
        has_prior = jnp.broadcast_to((block_index > 0) | (shard_index > 0), (QB, QB))
        visible = jnp.concatenate(
            [jnp.ones((QB, SEL * TILE), dtype=bool), has_prior, causal], axis=1
        )
        masked = jnp.where(visible, scores, NEG_FILL)
        row_top = jnp.max(masked, axis=3, keepdims=True)
        exponent = jnp.exp(masked - row_top)
        row_total = jnp.sum(exponent, axis=3)
        return (exponent.astype(jnp.bfloat16), row_total)

    def block_output(block_index, weights, row_total, got_values):
        all_values = jnp.concatenate(
            [remote_part(block_index, got_values), local_part(block_index, v_rows, prior_values)],
            axis=1,
        )
        weighted = jnp.einsum(
            "hgqk,hkd->qhgd", weights, all_values, preferred_element_type=jnp.float32
        )
        result = weighted / jnp.transpose(row_total, (2, 0, 1))[..., None]
        return result.astype(jnp.bfloat16).reshape(QB, kv_here * group_size * HD)

    block_ids = jnp.arange(blocks_here)
    got_keys, got_values = (
        lax.all_to_all(send_keys, "seq", split_axis=0, concat_axis=0, tiled=True),
        lax.all_to_all(send_values, "seq", split_axis=0, concat_axis=0, tiled=True),
    )

    def whole_block(block_index):
        weights, row_total = block_weights(block_index, got_keys)
        return block_output(block_index, weights, row_total, got_values)

    outputs = lax.map(whole_block, block_ids)
    attended = outputs.reshape(rows_here, kv_here * group_size * HD)
    return lax.all_to_all(attended, "head", split_axis=0, concat_axis=1, tiled=True)


def solution(mesh):
    return jax.shard_map(
        on_device,
        mesh=mesh,
        in_specs=(
            P(("seq", "head"), None),
            P(("seq", "head"), None),
            P(("seq", "head"), None),
            P("seq", "head"),
            P("seq", "head"),
            P("seq", "head", None),
        ),
        out_specs=P(("seq", "head"), None),
        check_vma=False,
    )
```

profile of v0, /device:TPU:14, one launch (start us, length us, event | category | flops | bytes accessed | tf_op | source)
XLA Modules:
  0.0 396.6 jit_solution(17193188782176240120)
XLA Ops:
  1.6 10.3 %all-to-all-start.1 = ((bf16[64,8,128]{2,0,1:T(8,128)(2,1)}), bf16[64,8,128]{2,0,1:T(8,128)(2,1)S(1)}, u32[]{:S(2)}, u32[]{:S(2)}) async-start(bf16[64,8,128]{2,0,1:T(8,128)(2,1)} %copy_bitcast_fusion.2), calls=%async_computation.1 | async-start | bytes 262144 | tf_op jit(solution)/shard_map/all_to_all | solution.py:37
  12.0 49.1 %all_gather.3 = s32[256,1,12]{2,1,0:T(1,128)S(1)} all-gather(s32[4,1,12]{2,1,0:T(1,128)} %param.13), channel_id=1, replica_groups=mesh['seq'=64,'head'=8] {'seq'}, dimensions={0}, use_global_device_ids=true | all-gather | bytes 12480 | tf_op jit(solution)/shard_map/all_gather | solution.py:56
  63.1 1.9 copy.90
  67.0 7.2 %all-to-all-start.3 = ((bf16[64,8,128]{2,0,1:T(8,128)(2,1)}), bf16[64,8,128]{2,0,1:T(8,128)(2,1)S(1)}, u32[]{:S(2)}, u32[]{:S(2)}) async-start(bf16[64,8,128]{2,0,1:T(8,128)(2,1)} %copy_bitcast_fusion.1), calls=%async_computation.3 | async-start | bytes 262144 | tf_op jit(solution)/shard_map/all_to_all | solution.py:36
  74.2 9.6 %all-to-all-done.3 = bf16[64,8,128]{2,0,1:T(8,128)(2,1)S(1)} async-done(((bf16[64,8,128]{2,0,1:T(8,128)(2,1)}), bf16[64,8,128]{2,0,1:T(8,128)(2,1)S(1)}, u32[]{:S(2)}, u32[]{:S(2)}) %all-to-all-start.3) | async-done | bytes 131104 | tf_op jit(solution)/shard_map/all_to_all | solution.py:36
  83.8 3.5 all-to-all-start.4
  87.6 3.1 gather_fusion.2
  90.6 3.0 gather_fusion.3
  93.8 5.8 %broadcast_select_fusion = (bf16[64,1,2,128,128]{4,3,2,1,0:T(8,128)(2,1)}, bf16[64,1,2,128,128]{4,3,2,1,0:T(8,128)(2,1)}) fusion(bf16[64,1,2,128,128]{4,3,2,1,0:T(8,128)(2,1)} %bitcast.146, pred[64,2]{1,0:T(8,128)(4,1)S(1)} %copy.70, bf16[64,1,2,128,128]{4,3,2,1,0:T(8,128)(2,1)} %bitcast.145), kind=kLoop, calls=%fused_computation.42 | loop fusion | flops 4194304 | bytes 16777344 | tf_op jit(solution)/shard_map/jit(_where)/select_n | solution.py:71
  99.6 4.4 %all-to-all-done.4 = bf16[64,8,512]{2,0,1:T(8,128)(2,1)S(1)} async-done(((bf16[64,8,512]{2,0,1:T(8,128)(2,1)}), bf16[64,8,512]{2,0,1:T(8,128)(2,1)S(1)}, u32[]{:S(2)}, u32[]{:S(2)}) %all-to-all-start.4) | async-done | bytes 524320 | tf_op jit(solution)/shard_map/all_to_all | solution.py:35
  104.0 104.5 %all_to_all.86 = bf16[64,1,2,128,128]{4,3,2,1,0:T(8,128)(2,1)} all-to-all(bf16[64,1,2,128,128]{4,3,2,1,0:T(8,128)(2,1)} %get-tuple-element.300), channel_id=1, replica_groups=mesh['seq'=64,'head'=8] {'seq'}, dimensions={0} | all-to-all | bytes 8388608 | tf_op jit(solution)/shard_map/all_to_all | solution.py:124
  208.5 6.6 %all-to-all-start.2 = ((bf16[64,1,2,128,128]{4,3,2,1,0:T(8,128)(2,1)}), bf16[64,1,2,128,128]{4,3,2,1,0:T(8,128)(2,1)}, u32[]{:S(2)}, u32[]{:S(2)}) async-start(bf16[64,1,2,128,128]{4,3,2,1,0:T(8,128)(2,1)} %get-tuple-element.299), calls=%async_computation.2 | async-start | bytes 8388608 | tf_op jit(solution)/shard_map/all_to_all | solution.py:123
  216.1 2.1 collective-permute-start
  218.2 3.4 collective-permute-start.1
  221.7 4.7 %collective-permute-done = bf16[128,128]{1,0:T(8,128)(2,1)S(1)} collective-permute-done((bf16[128,128]{1,0:T(8,128)(2,1)S(1)}, bf16[128,128]{1,0:T(8,128)(2,1)S(1)}, u32[]{:S(2)}, u32[]{:S(2)}) %collective-permute-start) | collective-permute-done | bytes 32800 | tf_op jit(solution)/shard_map/ppermute | solution.py:19
  227.0 83.4 %all-to-all-done.2 = bf16[64,1,2,128,128]{4,3,2,1,0:T(8,128)(2,1)} async-done(((bf16[64,1,2,128,128]{4,3,2,1,0:T(8,128)(2,1)}), bf16[64,1,2,128,128]{4,3,2,1,0:T(8,128)(2,1)}, u32[]{:S(2)}, u32[]{:S(2)}) %all-to-all-start.2) | async-done | bytes 4194336 | tf_op jit(solution)/shard_map/all_to_all | solution.py:123
  310.4 65.0 %while.13 = (s32[]{:T(128)}, bf16[4,128,512]{2,1,0:T(8,128)(2,1)S(1)}, s32[4]{0:T(128)S(1)}, s32[1,48]{1,0:T(1,128)S(1)}, s32[1,48]{1,0:T(1,128)S(1)}, /*index=5...) while((s32[]{:T(128)}, ...), condition=%wide.region_8.9_spmd.clone, body=%wide.region_5.8_spmd.clone.sunk | while | flops 478692352 | bytes 31508588 | solution.py:131
  313.6 2.9 gather_fusion
  318.2 1.9 copy-done.1
  320.7 2.9 gather_fusion.1
  323.7 2.8 fusion.49
  329.8 2.9 gather_fusion
  336.9 2.9 gather_fusion.1
  340.0 2.8 fusion.49
  346.1 2.9 gather_fusion
  350.7 1.9 copy-done.1
  353.2 2.9 gather_fusion.1
  356.2 2.8 fusion.49
  362.3 2.9 gather_fusion
  369.4 2.9 gather_fusion.1
  372.5 2.8 fusion.49
  375.4 20.3 %all_to_all.87 = bf16[8,64,512]{2,1,0:T(8,128)(2,1)S(1)} all-to-all(bf16[8,64,512]{2,1,0:T(8,128)(2,1)S(1)} %bitcast.157), channel_id=1, replica_groups=mesh['seq'=64,'head'=8] {'head'}, dimensions={0} | all-to-all | bytes 1048576 | tf_op jit(solution)/shard_map/all_to_all | solution.py:133
  (130 shorter events, 23.9 us)
Async XLA Ops:
  0.0 87.5 %copy-start = (bf16[2048,128]{1,0:T(8,128)(2,1)S(1)}, bf16[2048,128]{1,0:T(8,128)(2,1)}, u32[]{:S(2)}) copy-start(bf16[2048,128]{1,0:T(8,128)(2,1)} %param.12) | copy-start | bytes 1572868
  1.6 65.4 %all-to-all-start.1 = ((bf16[64,8,128]{2,0,1:T(8,128)(2,1)}), bf16[64,8,128]{2,0,1:T(8,128)(2,1)S(1)}, u32[]{:S(2)}, u32[]{:S(2)}) async-start(bf16[64,8,128]{2,0,1:T(8,128)(2,1)} %copy_bitcast_fusion.2), calls=%async_computation.1 | async-start | bytes 262144 | tf_op jit(solution)/shard_map/all_to_all | solution.py:37
  67.0 16.8 %all-to-all-start.3 = ((bf16[64,8,128]{2,0,1:T(8,128)(2,1)}), bf16[64,8,128]{2,0,1:T(8,128)(2,1)S(1)}, u32[]{:S(2)}, u32[]{:S(2)}) async-start(bf16[64,8,128]{2,0,1:T(8,128)(2,1)} %copy_bitcast_fusion.1), calls=%async_computation.3 | async-start | bytes 262144 | tf_op jit(solution)/shard_map/all_to_all | solution.py:36
  83.8 20.2 %all-to-all-start.4 = ((bf16[64,8,512]{2,0,1:T(8,128)(2,1)}), bf16[64,8,512]{2,0,1:T(8,128)(2,1)S(1)}, u32[]{:S(2)}, u32[]{:S(2)}) async-start(bf16[64,8,512]{2,0,1:T(8,128)(2,1)} %bitcast.99), calls=%async_computation.4 | async-start | bytes 1048576 | tf_op jit(solution)/shard_map/all_to_all | solution.py:35
  87.6 3.1 copy-start.2
  208.5 6.6 %copy-start.3 = (s32[4,1,12]{2,1,0:T(1,128)S(1)}, s32[4,1,12]{2,1,0:T(1,128)}, u32[]{:S(2)}) copy-start(s32[4,1,12]{2,1,0:T(1,128)} %param.13) | copy-start | bytes 580
  208.5 102.0 %all-to-all-start.2 = ((bf16[64,1,2,128,128]{4,3,2,1,0:T(8,128)(2,1)}), bf16[64,1,2,128,128]{4,3,2,1,0:T(8,128)(2,1)}, u32[]{:S(2)}, u32[]{:S(2)}) async-start(bf16[64,1,2,128,128]{4,3,2,1,0:T(8,128)(2,1)} %get-tuple-element.299), calls=%async_computation.2 | async-start | bytes 8388608 | tf_op jit(solution)/shard_map/all_to_all | solution.py:123
  216.1 10.3 %collective-permute-start = (bf16[128,128]{1,0:T(8,128)(2,1)S(1)}, bf16[128,128]{1,0:T(8,128)(2,1)S(1)}, u32[]{:S(2)}, u32[]{:S(2)}) collective-permute-start(bf16[128,128]{1,0:T(8,128)(2,1)S(1)} %bitcast.159), channel_id=1, source_target_pairs={{0,8},{8,16},{16,24},{24,32},{32,40},{40,48},{48,56},{56,64},{64,7... | collective-permute-start | bytes 98312 | tf_op jit(solution)/shard_map/ppermute | solution.py:19
  218.2 8.9 %collective-permute-start.1 = (bf16[128,128]{1,0:T(8,128)(2,1)S(1)}, bf16[128,128]{1,0:T(8,128)(2,1)S(1)}, u32[]{:S(2)}, u32[]{:S(2)}) collective-permute-start(bf16[128,128]{1,0:T(8,128)(2,1)S(1)} %bitcast.160), channel_id=1, source_target_pairs={{0,8},{8,16},{16,24},{24,32},{32,40},{40,48},{48,56},{56,64},{64,7... | collective-permute-start | bytes 98312 | tf_op jit(solution)/shard_map/ppermute | solution.py:19
  318.2 1.9 copy-start.1
  334.4 1.9 copy-start.1
  350.7 1.9 copy-start.1
  366.9 1.9 copy-start.1
where the time goes:
time: 398 us; the launch traced here: 397 us
  blocking collectives  174 us (44%)
  waiting for transfers between devices  103 us (26%)
  local copies, waits for them, and re-layouts  48.2 us (12%)
  starting transfers between devices  33 us (8%)
  matrix products  13.7 us (3%)
  other arithmetic  12.8 us (3%)
  loops' own time  12.1 us (3%)
    all_to_all x1, blocking collectives, on_device(): lax.all_to_all(send_values, 'seq', split_axis=0, concat_axis=0, tiled=True)  104 us
    all_to_all x1, waiting for transfers between devices, on_device(): lax.all_to_all(send_keys, 'seq', split_axis=0, concat_axis=0, tiled=True)  83.4 us
    all_gather x1, blocking collectives, on_device(): every_list = lax.all_gather(tile_lists, 'seq', axis=0, tiled=True)  49.1 us
    gather x8, local copies, waits for them, and re-layouts, remote_part(): received[block_owners, head_rows, block_ranks]  22.8 us
    all_to_all x1, blocking collectives, on_device(): lax.all_to_all(attended, 'head', split_axis=0, concat_axis=1, tiled=True)  20.3 us
    another operation x1, loops' own time, on_device(): outputs = lax.map(whole_block, block_ids)  12.1 us
    dot_general x4, matrix products, block_output(): jnp.einsum('hgqk,hkd->qhgd', weights, all_values, preferred_element_type=...  11.2 us
    all_to_all x1, starting transfers between devices, on_device(): lax.all_to_all(new_values, 'head', split_axis=1, concat_axis=0, tiled=True)  10.3 us
  transfers between devices with their start and end apart: 6, of which 5 were waited for; matrix products, arithmetic and copies ran while one was open for 5% of the time, Pallas kernels for 0%

commit v1 on v0

--- a/solution.py
+++ b/solution.py
@@ -11,6 +11,11 @@
 TILE = 128
 SEL = 12
 NEG_FILL = -1e30
+
+
+def swapped_in(value, mesh_axis, dim):
+    sent = jnp.stack([value] * lax.axis_size(mesh_axis))
+    return jnp.concatenate(lax.all_to_all(sent, mesh_axis, 0, 0), axis=dim)
 
 
 def passed_along(block, axis, distance):
@@ -53,7 +58,7 @@
     pair_tiles = jnp.transpose(tile_lists, (1, 0, 2)).reshape(kv_here, pair_total)
     owners = pair_tiles // tiles_here
     pair_rank, first_seen = pair_ranks(owners, pair_tiles)
-    every_list = lax.all_gather(tile_lists, "seq", axis=0, tiled=True)
+    every_list = swapped_in(tile_lists, "seq", 0)
     every_pair = jnp.transpose(
         every_list.reshape(shards, blocks_here, kv_here, SEL), (0, 2, 1, 3)
     ).reshape(shards, kv_here, pair_total)

time: 398 us -> 366 us (0.920)
  blocking collectives: 174 us -> 125 us
  waiting for transfers between devices: 103 us -> 111 us
  starting transfers between devices: 33 us -> 39.7 us
    all_gather x1 -> x0, blocking collectives: 49.1 us -> none  [on_device(): every_list = lax.all_gather(tile_lists, 'seq', axis=0, tiled=True)]
    all_to_all x0 -> x1, starting transfers between devices: none -> 10.5 us  [swapped_in(): return jnp.concatenate(lax.all_to_all(sent, mesh_axis, 0, 0), axis=dim)]
    all_to_all x1, waiting for transfers between devices: 0.01 us -> 6.5 us  [on_device(): lax.all_to_all(new_values, 'head', split_axis=1, concat_axis=0, tiled=True)]
  transfers between devices with their start and end apart: 6 -> 7, of which waited for: 5 -> 7; matrix products, arithmetic and copies ran while one was open for 5% -> 6% of each run, Pallas kernels for 0% -> 0%
where the time goes in v1:
time: 366 us; the launch traced here: 364 us
  blocking collectives  125 us (34%)
  waiting for transfers between devices  111 us (30%)
  local copies, waits for them, and re-layouts  49.7 us (14%)
  starting transfers between devices  39.7 us (11%)
  matrix products  13.7 us (4%)
  other arithmetic  12.8 us (3%)
  loops' own time  12.1 us (3%)
    all_to_all x1, blocking collectives, on_device(): lax.all_to_all(send_values, 'seq', split_axis=0, concat_axis=0, tiled=True)  104 us
    all_to_all x1, waiting for transfers between devices, on_device(): lax.all_to_all(send_keys, 'seq', split_axis=0, concat_axis=0, tiled=True)  83.4 us
    gather x8, local copies, waits for them, and re-layouts, remote_part(): received[block_owners, head_rows, block_ranks]  22.8 us
    all_to_all x1, blocking collectives, on_device(): lax.all_to_all(attended, 'head', split_axis=0, concat_axis=1, tiled=True)  21.7 us
    another operation x1, loops' own time, on_device(): outputs = lax.map(whole_block, block_ids)  12.1 us
    dot_general x4, matrix products, block_output(): jnp.einsum('hgqk,hkd->qhgd', weights, all_values, preferred_element_type=...  11.2 us
    all_to_all x1, starting transfers between devices, swapped_in(): return jnp.concatenate(lax.all_to_all(sent, mesh_axis, 0, 0), axis=dim)  10.5 us
    all_to_all x1, starting transfers between devices, on_device(): lax.all_to_all(new_values, 'head', split_axis=1, concat_axis=0, tiled=True)  10.3 us
  transfers between devices with their start and end apart: 7, of which 7 were waited for; matrix products, arithmetic and copies ran while one was open for 6% of the time, Pallas kernels for 0%

profile of v1, /device:TPU:14, one launch (start us, length us, event | category | flops | bytes accessed | tf_op | source)
XLA Modules:
  0.0 364.2 jit_solution(3538130317850450844)
XLA Ops:
  1.5 10.5 %all-to-all-start = ((s32[64,4,1,12]{3,2,1,0:T(1,128)}), s32[64,4,1,12]{3,2,1,0:T(1,128)S(1)}, u32[]{:S(2)}, u32[]{:S(2)}) async-start(s32[64,4,1,12]{3,2,1,0:T(1,128)} %stack.2), calls=%async_computation | async-start | bytes 262144 | tf_op jit(solution)/shard_map/all_to_all | solution.py:18
  15.1 1.9 copy.115
  17.0 3.8 %all-to-all-done = s32[64,4,1,12]{3,2,1,0:T(1,128)S(1)} async-done(((s32[64,4,1,12]{3,2,1,0:T(1,128)}), s32[64,4,1,12]{3,2,1,0:T(1,128)S(1)}, u32[]{:S(2)}, u32[]{:S(2)}) %all-to-all-start) | async-done | bytes 12320 | tf_op jit(solution)/shard_map/all_to_all | solution.py:18
  20.9 10.3 %all-to-all-start.2 = ((bf16[64,8,128]{2,0,1:T(8,128)(2,1)}), bf16[64,8,128]{2,0,1:T(8,128)(2,1)S(1)}, u32[]{:S(2)}, u32[]{:S(2)}) async-start(bf16[64,8,128]{2,0,1:T(8,128)(2,1)} %copy_bitcast_fusion.2), calls=%async_computation.2 | async-start | bytes 262144 | tf_op jit(solution)/shard_map/all_to_all | solution.py:42
  33.8 6.5 %all-to-all-done.2 = bf16[64,8,128]{2,0,1:T(8,128)(2,1)S(1)} async-done(((bf16[64,8,128]{2,0,1:T(8,128)(2,1)}), bf16[64,8,128]{2,0,1:T(8,128)(2,1)S(1)}, u32[]{:S(2)}, u32[]{:S(2)}) %all-to-all-start.2) | async-done | bytes 131104 | tf_op jit(solution)/shard_map/all_to_all | solution.py:42
  40.3 3.4 all-to-all-start.4
  43.7 9.0 %all-to-all-done.4 = bf16[64,8,128]{2,0,1:T(8,128)(2,1)S(1)} async-done(((bf16[64,8,128]{2,0,1:T(8,128)(2,1)}), bf16[64,8,128]{2,0,1:T(8,128)(2,1)S(1)}, u32[]{:S(2)}, u32[]{:S(2)}) %all-to-all-start.4) | async-done | bytes 131104 | tf_op jit(solution)/shard_map/all_to_all | solution.py:41
  52.6 3.5 all-to-all-start.5
  56.4 3.0 gather_fusion.3
  59.4 3.1 gather_fusion.2
  62.6 5.8 %broadcast_select_fusion = (bf16[64,1,2,128,128]{4,3,2,1,0:T(8,128)(2,1)}, bf16[64,1,2,128,128]{4,3,2,1,0:T(8,128)(2,1)}) fusion(bf16[64,1,2,128,128]{4,3,2,1,0:T(8,128)(2,1)} %bitcast.146, pred[64,2]{1,0:T(8,128)(4,1)S(1)} %copy.94, bf16[64,1,2,128,128]{4,3,2,1,0:T(8,128)(2,1)} %bitcast.147), kind=kLoop, calls=%fused_computation.42 | loop fusion | flops 4194304 | bytes 16777344 | tf_op jit(solution)/shard_map/jit(_where)/select_n | solution.py:76
  68.4 2.6 all-to-all-done.5
  71.1 103.6 %all_to_all.91 = bf16[64,1,2,128,128]{4,3,2,1,0:T(8,128)(2,1)} all-to-all(bf16[64,1,2,128,128]{4,3,2,1,0:T(8,128)(2,1)} %get-tuple-element.300), channel_id=1, replica_groups=mesh['seq'=64,'head'=8] {'seq'}, dimensions={0} | all-to-all | bytes 8388608 | tf_op jit(solution)/shard_map/all_to_all | solution.py:129
  174.6 6.6 %all-to-all-start.3 = ((bf16[64,1,2,128,128]{4,3,2,1,0:T(8,128)(2,1)}), bf16[64,1,2,128,128]{4,3,2,1,0:T(8,128)(2,1)}, u32[]{:S(2)}, u32[]{:S(2)}) async-start(bf16[64,1,2,128,128]{4,3,2,1,0:T(8,128)(2,1)} %get-tuple-element.299), calls=%async_computation.3 | async-start | bytes 8388608 | tf_op jit(solution)/shard_map/all_to_all | solution.py:128
  182.3 2.1 collective-permute-start
  184.3 3.4 collective-permute-start.1
  187.9 4.7 %collective-permute-done = bf16[128,128]{1,0:T(8,128)(2,1)S(1)} collective-permute-done((bf16[128,128]{1,0:T(8,128)(2,1)S(1)}, bf16[128,128]{1,0:T(8,128)(2,1)S(1)}, u32[]{:S(2)}, u32[]{:S(2)}) %collective-permute-start) | collective-permute-done | bytes 32800 | tf_op jit(solution)/shard_map/ppermute | solution.py:24
  193.2 83.4 %all-to-all-done.3 = bf16[64,1,2,128,128]{4,3,2,1,0:T(8,128)(2,1)} async-done(((bf16[64,1,2,128,128]{4,3,2,1,0:T(8,128)(2,1)}), bf16[64,1,2,128,128]{4,3,2,1,0:T(8,128)(2,1)}, u32[]{:S(2)}, u32[]{:S(2)}) %all-to-all-start.3) | async-done | bytes 4194336 | tf_op jit(solution)/shard_map/all_to_all | solution.py:128
  276.6 65.0 %while.13 = (s32[]{:T(128)}, bf16[4,128,512]{2,1,0:T(8,128)(2,1)S(1)}, s32[4]{0:T(128)S(1)}, s32[1,48]{1,0:T(1,128)S(1)}, s32[1,48]{1,0:T(1,128)S(1)}, /*index=5...) while((s32[]{:T(128)}, ...), condition=%wide.region_8.9_spmd.clone, body=%wide.region_5.8_spmd.clone.sunk | while | flops 478692352 | bytes 31508588 | solution.py:136
  279.7 2.9 gather_fusion
  286.8 2.9 gather_fusion.1
  289.9 2.8 fusion.49
  296.0 2.9 gather_fusion
  303.1 2.9 gather_fusion.1
  306.1 2.8 fusion.49
  312.2 2.9 gather_fusion
  319.3 2.9 gather_fusion.1
  322.4 2.8 fusion.49
  328.5 2.9 gather_fusion
  335.6 2.9 gather_fusion.1
  338.6 2.8 fusion.49
  341.6 21.7 %all_to_all.92 = bf16[8,64,512]{2,1,0:T(8,128)(2,1)S(1)} all-to-all(bf16[8,64,512]{2,1,0:T(8,128)(2,1)S(1)} %bitcast.158), channel_id=1, replica_groups=mesh['seq'=64,'head'=8] {'head'}, dimensions={0} | all-to-all | bytes 1048576 | tf_op jit(solution)/shard_map/all_to_all | solution.py:138
  (132 shorter events, 29.1 us)
Async XLA Ops:
  0.0 56.4 %copy-start = (bf16[2048,128]{1,0:T(8,128)(2,1)S(1)}, bf16[2048,128]{1,0:T(8,128)(2,1)}, u32[]{:S(2)}) copy-start(bf16[2048,128]{1,0:T(8,128)(2,1)} %param.11) | copy-start | bytes 1572868
  1.5 19.4 %all-to-all-start = ((s32[64,4,1,12]{3,2,1,0:T(1,128)}), s32[64,4,1,12]{3,2,1,0:T(1,128)S(1)}, u32[]{:S(2)}, u32[]{:S(2)}) async-start(s32[64,4,1,12]{3,2,1,0:T(1,128)} %stack.2), calls=%async_computation | async-start | bytes 262144 | tf_op jit(solution)/shard_map/all_to_all | solution.py:18
  20.9 19.4 %all-to-all-start.2 = ((bf16[64,8,128]{2,0,1:T(8,128)(2,1)}), bf16[64,8,128]{2,0,1:T(8,128)(2,1)S(1)}, u32[]{:S(2)}, u32[]{:S(2)}) async-start(bf16[64,8,128]{2,0,1:T(8,128)(2,1)} %copy_bitcast_fusion.2), calls=%async_computation.2 | async-start | bytes 262144 | tf_op jit(solution)/shard_map/all_to_all | solution.py:42
  40.3 12.4 %all-to-all-start.4 = ((bf16[64,8,128]{2,0,1:T(8,128)(2,1)}), bf16[64,8,128]{2,0,1:T(8,128)(2,1)S(1)}, u32[]{:S(2)}, u32[]{:S(2)}) async-start(bf16[64,8,128]{2,0,1:T(8,128)(2,1)} %copy_bitcast_fusion.1), calls=%async_computation.4 | async-start | bytes 262144 | tf_op jit(solution)/shard_map/all_to_all | solution.py:41
  52.6 18.5 %all-to-all-start.5 = ((bf16[64,8,512]{2,0,1:T(8,128)(2,1)}), bf16[64,8,512]{2,0,1:T(8,128)(2,1)S(1)}, u32[]{:S(2)}, u32[]{:S(2)}) async-start(bf16[64,8,512]{2,0,1:T(8,128)(2,1)} %bitcast.100), calls=%async_computation.5 | async-start | bytes 1048576 | tf_op jit(solution)/shard_map/all_to_all | solution.py:40
  56.4 3.0 copy-start.2
  174.6 6.6 %copy-start.3 = (s32[4,1,12]{2,1,0:T(1,128)S(1)}, s32[4,1,12]{2,1,0:T(1,128)}, u32[]{:S(2)}) copy-start(s32[4,1,12]{2,1,0:T(1,128)} %param.13) | copy-start | bytes 580
  174.6 102.0 %all-to-all-start.3 = ((bf16[64,1,2,128,128]{4,3,2,1,0:T(8,128)(2,1)}), bf16[64,1,2,128,128]{4,3,2,1,0:T(8,128)(2,1)}, u32[]{:S(2)}, u32[]{:S(2)}) async-start(bf16[64,1,2,128,128]{4,3,2,1,0:T(8,128)(2,1)} %get-tuple-element.299), calls=%async_computation.3 | async-start | bytes 8388608 | tf_op jit(solution)/shard_map/all_to_all | solution.py:128
  182.3 10.3 %collective-permute-start = (bf16[128,128]{1,0:T(8,128)(2,1)S(1)}, bf16[128,128]{1,0:T(8,128)(2,1)S(1)}, u32[]{:S(2)}, u32[]{:S(2)}) collective-permute-start(bf16[128,128]{1,0:T(8,128)(2,1)S(1)} %bitcast.160), channel_id=1, source_target_pairs={{0,8},{8,16},{16,24},{24,32},{32,40},{40,48},{48,56},{56,64},{64,7... | collective-permute-start | bytes 98312 | tf_op jit(solution)/shard_map/ppermute | solution.py:24
  184.3 8.9 %collective-permute-start.1 = (bf16[128,128]{1,0:T(8,128)(2,1)S(1)}, bf16[128,128]{1,0:T(8,128)(2,1)S(1)}, u32[]{:S(2)}, u32[]{:S(2)}) collective-permute-start(bf16[128,128]{1,0:T(8,128)(2,1)S(1)} %bitcast.161), channel_id=1, source_target_pairs={{0,8},{8,16},{16,24},{24,32},{32,40},{40,48},{48,56},{56,64},{64,7... | collective-permute-start | bytes 98312 | tf_op jit(solution)/shard_map/ppermute | solution.py:24
  284.3 1.9 copy-start.1
  300.6 1.9 copy-start.1
  316.8 1.9 copy-start.1
  333.1 1.9 copy-start.1
